TPU v7x, 32 devices: a whole 2x2x4 slice. The times are simulated.
32 devices in a mesh: rep: 4 (over x, core), fsdp: 4 (over z), seq: 2 (over y).
Axes of the slice: x: 2, y: 2, z: 4, core: 2. Of those that a mesh axis runs over, the one named last changes fastest.
Arguments:
- tokens: bfloat16 [16, 592, 1024], P(('rep', 'fsdp'), 'seq'), may hold values from -6 to 6
- slot_mask: int32 [16], P(('rep', 'fsdp')), may hold values 0 or 1
- cotangent: bfloat16 [16, 592, 1024], P(('rep', 'fsdp'), 'seq'), may hold values from -6 to 6
- w_qkv: float32 [1024, 3072], P('fsdp'), may hold values from -0.25 to 0.25
- w_out: float32 [1024, 1024], P('fsdp'), may hold values from -0.75 to 0.75
- w_fc1: float32 [1024, 4096], P('fsdp'), may hold values from -0.1875 to 0.1875
- w_fc2: float32 [4096, 1024], P('fsdp'), may hold values from -0.125 to 0.125
- ln_gains: float32 [2, 1024], P(None, 'fsdp'), may hold values from 0.5 to 1.5
- biases: float32 [6, 1024], P(None, 'fsdp'), may hold values from -2 to 2
- fc1_bias: float32 [4096], P('fsdp'), may hold values from -2 to 2
Outputs:
- output: bfloat16 [16, 592, 1024], P(('rep', 'fsdp'), 'seq')
- grad_tokens: bfloat16 [16, 592, 1024], P(('rep', 'fsdp'), 'seq')
- grad_w_qkv: float32 [1024, 3072], P('fsdp')
- grad_w_out: float32 [1024, 1024], P('fsdp')
- grad_w_fc1: float32 [1024, 4096], P('fsdp')
- grad_w_fc2: float32 [4096, 1024], P('fsdp')
- grad_ln_gains: float32 [2, 1024], P(None, 'fsdp')
- grad_biases: float32 [6, 1024], P(None, 'fsdp')
- grad_fc1_bias: float32 [4096], P('fsdp')
All inputs are finite; a program needn't handle non-finite values. No bound on the sum of `slot_mask` on one device may be relied on, other than what follows from the above.
Results may differ from a plain program's by a relative error of at most 0.02.
The roundings to bfloat16 on the way count: a program that leaves them out, or rounds other values in their place, can miss the bound.
Values may be sent and summed in bfloat16 or wider, within the bound.
No kernel may reach another device: no remote copies, remote signals or barrier semaphores. Data moves between devices by JAX's collectives and lax.ppermute only.
A program may use at most 192 MiB of HBM per device.

v0:
```python
import jax
import jax.numpy as jnp
from jax import lax
from jax.sharding import PartitionSpec as P

HEADS = 16
HEAD_DIM = 64
IMG_TOK = 577
EPSILON = 1e-05
NEGATIVE = -1e30


def normalize(inputs, gain_row, shift_row):
    center = inputs - jnp.mean(inputs, axis=-1, keepdims=True)
    inverse = lax.rsqrt(jnp.mean(center * center, axis=-1, keepdims=True) + EPSILON)
    scaled = center * inverse
    return (scaled * gain_row + shift_row, scaled, inverse)


def norm_back(grad_in, scaled, inverse, gain_row):
    weighted = grad_in * gain_row
    return inverse * (
        weighted
        - jnp.mean(weighted, axis=-1, keepdims=True)
        - scaled * jnp.mean(weighted * scaled, axis=-1, keepdims=True)
    )


def across_rows(left_rows, right_rows):
    return lax.dot_general(
        left_rows, right_rows, (((0,), (0,)), ((), ())), preferred_element_type=jnp.float32
    )


def times_transposed(left_rows, right_rows):
    return lax.dot_general(
        left_rows, right_rows, (((1,), (1,)), ((), ())), preferred_element_type=jnp.float32
    )


def split_heads(matrix):
    return matrix.reshape(matrix.shape[0], HEADS, HEAD_DIM)


def masked_scores(query_rows, key_rows):
    scores = jnp.einsum(
        "qhd,khd->hqk",
        split_heads(query_rows),
        split_heads(key_rows),
        preferred_element_type=jnp.float32,
    )
    valid_keys = jnp.arange(key_rows.shape[0]) < IMG_TOK
    return jnp.where(valid_keys[None, None, :], scores, NEGATIVE)


def attend_slot(blocks_in):
    query_rows, key_rows, value_rows = blocks_in
    scores = masked_scores(query_rows, key_rows)
    highest = jnp.max(scores, axis=-1, keepdims=True)
    exponent = jnp.exp(scores - highest)
    total_sum = jnp.sum(exponent, axis=-1, keepdims=True)
    weights = (exponent / total_sum).astype(jnp.bfloat16)
    mixed_rows = jnp.einsum(
        "hqk,khd->qhd", weights, split_heads(value_rows), preferred_element_type=jnp.float32
    )
    return (mixed_rows.reshape(query_rows.shape[0], -1), highest + jnp.log(total_sum))


def attend_back(blocks_in):
    query_rows, key_rows, value_rows, log_total, grad_rows = blocks_in
    scores = masked_scores(query_rows, key_rows)
    probability = jnp.exp(scores - log_total)
    grad_heads = split_heads(grad_rows)
    grad_probs = jnp.einsum(
        "qhd,khd->hqk", grad_heads, split_heads(value_rows), preferred_element_type=jnp.float32
    )
    inner_sum = jnp.sum(probability * grad_probs, axis=-1, keepdims=True)
    grad_scores = (probability * (grad_probs - inner_sum)).astype(jnp.bfloat16)
    grad_query = jnp.einsum(
        "hqk,khd->qhd", grad_scores, split_heads(key_rows), preferred_element_type=jnp.float32
    )
    grad_key = jnp.einsum(
        "hqk,qhd->khd", grad_scores, split_heads(query_rows), preferred_element_type=jnp.float32
    )
    grad_value = jnp.einsum(
        "hqk,qhd->khd",
        probability.astype(jnp.bfloat16),
        grad_heads,
        preferred_element_type=jnp.float32,
    )
    key_count = key_rows.shape[0]
    return (
        grad_query.reshape(query_rows.shape[0], -1),
        grad_key.reshape(key_count, -1),
        grad_value.reshape(key_count, -1),
    )


def on_device(tokens, slot_mask, cotangent, w_qkv, w_out, w_fc1, w_fc2, ln_gains, biases, fc1_bias):
    slot_count, row_count, feature_width = tokens.shape
    low_qkv = w_qkv.astype(jnp.bfloat16)
    low_out = w_out.astype(jnp.bfloat16)
    low_fc1 = w_fc1.astype(jnp.bfloat16)
    low_fc2 = w_fc2.astype(jnp.bfloat16)
    low_gains = ln_gains.astype(jnp.bfloat16)
    low_biases = biases.astype(jnp.bfloat16)
    low_fc1_bias = fc1_bias.astype(jnp.bfloat16)
    gathered = (
        lax.all_gather(low_qkv, "fsdp", axis=0, tiled=True),
        lax.all_gather(low_out, "fsdp", axis=0, tiled=True),
        lax.all_gather(low_fc1, "fsdp", axis=0, tiled=True),
        lax.all_gather(low_fc2, "fsdp", axis=0, tiled=True),
        lax.all_gather(low_gains, "fsdp", axis=1, tiled=True),
        lax.all_gather(low_biases, "fsdp", axis=1, tiled=True),
        lax.all_gather(low_fc1_bias, "fsdp", axis=0, tiled=True),
    )
    big_qkv, big_out, big_fc1, big_fc2, gain_rows, bias_rows, fc1_shift = gathered
    gain_values = gain_rows.astype(jnp.float32)
    shift_values = bias_rows.astype(jnp.float32)
    hidden_shift = fc1_shift.astype(jnp.float32)
    head_scale = HEAD_DIM ** (-0.5)
    positions = lax.axis_index("seq") * row_count + jnp.arange(row_count)
    keep_mask = (
        slot_mask.astype(jnp.float32)[:, None] * (positions < IMG_TOK).astype(jnp.float32)[None, :]
    )
    keep_mask = keep_mask.reshape(-1, 1)
    inputs = tokens.astype(jnp.float32).reshape(-1, feature_width)
    normed_full, scaled_one, inverse_one = normalize(inputs, gain_values[0], shift_values[0])
    normed = normed_full.astype(jnp.bfloat16)
    joined = jnp.dot(normed, big_qkv, preferred_element_type=jnp.float32)
    queries = ((joined[:, :feature_width] + shift_values[1]) * head_scale).astype(jnp.bfloat16)
    keys_local = (
        joined[:, feature_width : 2 * feature_width]
        .astype(jnp.bfloat16)
        .reshape(slot_count, row_count, feature_width)
    )
    values_local = (
        (joined[:, 2 * feature_width :] + shift_values[2])
        .astype(jnp.bfloat16)
        .reshape(slot_count, row_count, feature_width)
    )
    slot_queries = queries.reshape(slot_count, row_count, feature_width)
    keys_all, values_all = (
        lax.all_gather(keys_local, "seq", axis=1, tiled=True),
        lax.all_gather(values_local, "seq", axis=1, tiled=True),
    )
    mixed_rows, log_total = lax.map(attend_slot, (slot_queries, keys_all, values_all))
    mixed_low = mixed_rows.reshape(-1, feature_width).astype(jnp.bfloat16)
    middle = inputs + (
        jnp.dot(mixed_low, big_out, preferred_element_type=jnp.float32) + shift_values[3]
    )
    normed_two_full, scaled_two, inverse_two = normalize(middle, gain_values[1], shift_values[4])
    normed_two = normed_two_full.astype(jnp.bfloat16)
    hidden = jnp.dot(normed_two, big_fc1, preferred_element_type=jnp.float32) + hidden_shift
    gate_values = jax.nn.sigmoid(1.702 * hidden)
    active = (hidden * gate_values).astype(jnp.bfloat16)
    result = jnp.dot(active, big_fc2, preferred_element_type=jnp.float32) + shift_values[5]
    output = ((middle + result) * keep_mask).astype(jnp.bfloat16).reshape(tokens.shape)
    again = (
        lax.all_gather(low_qkv, "fsdp", axis=0, tiled=True),
        lax.all_gather(low_out, "fsdp", axis=0, tiled=True),
        lax.all_gather(low_fc1, "fsdp", axis=0, tiled=True),
        lax.all_gather(low_fc2, "fsdp", axis=0, tiled=True),
        lax.all_gather(low_gains, "fsdp", axis=1, tiled=True),
        lax.all_gather(low_biases, "fsdp", axis=1, tiled=True),
        lax.all_gather(low_fc1_bias, "fsdp", axis=0, tiled=True),
    )
    back_qkv, back_out, back_fc1, back_fc2, back_gain_rows = (
        again[0],
        again[1],
        again[2],
        again[3],
        again[4],
    )
    back_gains = back_gain_rows.astype(jnp.float32)
    incoming = cotangent.astype(jnp.float32).reshape(-1, feature_width) * keep_mask
    grad_result = incoming.astype(jnp.bfloat16)
    grad_fc2 = across_rows(active, grad_result)
    grad_shift_five = jnp.sum(grad_result.astype(jnp.float32), axis=0)
    grad_active = times_transposed(grad_result, back_fc2)
    grad_hidden = (
        grad_active * (gate_values + 1.702 * hidden * gate_values * (1.0 - gate_values))
    ).astype(jnp.bfloat16)
    grad_fc1 = across_rows(normed_two, grad_hidden)
    grad_hidden_shift = jnp.sum(grad_hidden.astype(jnp.float32), axis=0)
    grad_normed_two = times_transposed(grad_hidden, back_fc1)
    grad_gain_two = jnp.sum(grad_normed_two * scaled_two, axis=0)
    grad_shift_four = jnp.sum(grad_normed_two, axis=0)
    grad_middle = incoming + norm_back(grad_normed_two, scaled_two, inverse_two, back_gains[1])
    grad_branch = grad_middle.astype(jnp.bfloat16)
    grad_out = across_rows(mixed_low, grad_branch)
    grad_shift_three = jnp.sum(grad_branch.astype(jnp.float32), axis=0)
    grad_mixed = times_transposed(grad_branch, back_out).astype(jnp.bfloat16)
    grad_query, key_part, value_part = lax.map(
        attend_back,
        (
            slot_queries,
            keys_all,
            values_all,
            log_total,
            grad_mixed.reshape(slot_count, row_count, feature_width),
        ),
    )
    grad_keys, grad_values = (
        lax.psum_scatter(
            key_part.astype(jnp.bfloat16), "seq", scatter_dimension=1, tiled=True
        ).astype(jnp.float32),
        lax.psum_scatter(
            value_part.astype(jnp.bfloat16), "seq", scatter_dimension=1, tiled=True
        ).astype(jnp.float32),
    )
    query_grad_low = (grad_query.astype(jnp.bfloat16) * head_scale).reshape(-1, feature_width)
    key_grad_low = grad_keys.astype(jnp.bfloat16).reshape(-1, feature_width)
    value_grad_low = grad_values.astype(jnp.bfloat16).reshape(-1, feature_width)
    grad_joined = jnp.concatenate([query_grad_low, key_grad_low, value_grad_low], axis=1)
    grad_qkv = across_rows(normed, grad_joined)
    grad_shift_one = jnp.sum(query_grad_low.astype(jnp.float32), axis=0)
    grad_shift_two = jnp.sum(value_grad_low.astype(jnp.float32), axis=0)
    grad_normed = times_transposed(grad_joined, back_qkv)
    grad_gain_one = jnp.sum(grad_normed * scaled_one, axis=0)
    grad_shift_zero = jnp.sum(grad_normed, axis=0)
    grad_inputs = grad_middle + norm_back(grad_normed, scaled_one, inverse_one, back_gains[0])
    grad_tokens = grad_inputs.astype(jnp.bfloat16).reshape(tokens.shape)
    grad_gains = jnp.stack([grad_gain_one, grad_gain_two])
    grad_shifts = jnp.stack(
        [
            grad_shift_zero,
            grad_shift_one,
            grad_shift_two,
            grad_shift_three,
            grad_shift_four,
            grad_shift_five,
        ]
    )
    shards = (
        lax.psum_scatter(
            grad_qkv.astype(jnp.bfloat16), "fsdp", scatter_dimension=0, tiled=True
        ).astype(jnp.float32),
        lax.psum_scatter(
            grad_out.astype(jnp.bfloat16), "fsdp", scatter_dimension=0, tiled=True
        ).astype(jnp.float32),
        lax.psum_scatter(
            grad_fc1.astype(jnp.bfloat16), "fsdp", scatter_dimension=0, tiled=True
        ).astype(jnp.float32),
        lax.psum_scatter(
            grad_fc2.astype(jnp.bfloat16), "fsdp", scatter_dimension=0, tiled=True
        ).astype(jnp.float32),
        lax.psum_scatter(
            grad_gains.astype(jnp.bfloat16), "fsdp", scatter_dimension=1, tiled=True
        ).astype(jnp.float32),
        lax.psum_scatter(
            grad_shifts.astype(jnp.bfloat16), "fsdp", scatter_dimension=1, tiled=True
        ).astype(jnp.float32),
        lax.psum_scatter(
            grad_hidden_shift.astype(jnp.bfloat16), "fsdp", scatter_dimension=0, tiled=True
        ).astype(jnp.float32),
    )
    summed = (
        lax.psum(shards[0].astype(jnp.bfloat16), ("rep", "seq")).astype(jnp.float32),
        lax.psum(shards[1].astype(jnp.bfloat16), ("rep", "seq")).astype(jnp.float32),
        lax.psum(shards[2].astype(jnp.bfloat16), ("rep", "seq")).astype(jnp.float32),
        lax.psum(shards[3].astype(jnp.bfloat16), ("rep", "seq")).astype(jnp.float32),
        lax.psum(shards[4].astype(jnp.bfloat16), ("rep", "seq")).astype(jnp.float32),
        lax.psum(shards[5].astype(jnp.bfloat16), ("rep", "seq")).astype(jnp.float32),
        lax.psum(shards[6].astype(jnp.bfloat16), ("rep", "seq")).astype(jnp.float32),
    )
    return (
        output,
        grad_tokens,
        summed[0],
        summed[1],
        summed[2],
        summed[3],
        summed[4],
        summed[5],
        summed[6],
    )


def solution(mesh):
    return jax.shard_map(
        on_device,
        mesh=mesh,
        in_specs=(
            P(("rep", "fsdp"), "seq", None),
            P(("rep", "fsdp")),
            P(("rep", "fsdp"), "seq", None),
            P("fsdp", None),
            P("fsdp", None),
            P("fsdp", None),
            P("fsdp", None),
            P(None, "fsdp"),
            P(None, "fsdp"),
            P("fsdp"),
        ),
        out_specs=(
            P(("rep", "fsdp"), "seq", None),
            P(("rep", "fsdp"), "seq", None),
            P("fsdp", None),
            P("fsdp", None),
            P("fsdp", None),
            P("fsdp", None),
            P(None, "fsdp"),
            P(None, "fsdp"),
            P("fsdp"),
        ),
        check_vma=False,
    )
```

profile of v0, /device:TPU:0, one launch (start us, length us, event | category | flops | bytes accessed | tf_op | source)
XLA Modules:
  0.0 1236.4 jit_solution(1024592312134364579)
XLA Ops:
  7.3 3.3 convert_element_type.215
  10.7 12.6 %all_gather.32 = bf16[2,1024]{1,0:T(2,128)(2,1)S(1)} all-gather(bf16[2,256]{1,0:T(2,128)(2,1)S(1)} %convert_element_type.210), channel_id=1, replica_groups=mesh['rep'=4,'fsdp'=4,'seq'=2] {'fsdp'}, dimensions={1}, use_global_device_ids=true | all-gather | bytes 5120 | tf_op jit(solution)/shard_map/all_gather | solution.py:113
  23.3 14.3 %all_gather.33 = bf16[6,1024]{1,0:T(8,128)(2,1)S(1)} all-gather(bf16[6,256]{1,0:T(8,128)(2,1)S(1)} %convert_element_type.212), channel_id=1, replica_groups=mesh['rep'=4,'fsdp'=4,'seq'=2] {'fsdp'}, dimensions={1}, use_global_device_ids=true | all-gather | bytes 15360 | tf_op jit(solution)/shard_map/all_gather | solution.py:114
  38.1 90.8 %all-gather.9.cloned.1.call-done = bf16[1024,3072]{1,0:T(8,128)(2,1)} async-done(((bf16[256,3072]{1,0:T(8,128)(2,1)}), bf16[1024,3072]{1,0:T(8,128)(2,1)}) %all-gather.9.cloned.1.call-update) | async-done | bytes 6291472 | tf_op jit(solution)/shard_map/all_gather | solution.py:109
  128.9 5.0 fusion.53
  134.0 1.8 copy-done.8
  135.8 0.9 slice.67
  136.8 2.9 fusion.36
  139.7 0.9 convert_element_type.222
  140.7 4.1 convert_element_type.224
  144.9 3.8 convert_element_type.228
  149.5 11.9 all_gather.39
  161.8 1.9 copy.33
  163.7 19.9 %all-gather.17.cloned.1.call-done = bf16[592,1024]{1,0:T(8,128)(2,1)} async-done(((bf16[296,1024]{1,0:T(8,128)(2,1)}), bf16[592,1024]{1,0:T(8,128)(2,1)}) %all-gather.17.cloned.1.call-update) | async-done | bytes 1212432 | tf_op jit(solution)/shard_map/all_gather | solution.py:145
  183.6 2.4 copy.31
  186.0 2.2 select_reduce_fusion
  188.2 3.2 fusion
  191.5 1.7 copy-done
  193.1 4.5 fusion.20
  197.6 33.4 %all-gather.11.cloned.1.call-done = bf16[1024,1024]{1,0:T(8,128)(2,1)} async-done(((bf16[256,1024]{1,0:T(8,128)(2,1)}), bf16[1024,1024]{1,0:T(8,128)(2,1)}) %all-gather.11.cloned.1.call-update) | async-done | bytes 2097168 | tf_op jit(solution)/shard_map/all_gather | solution.py:110
  231.0 2.8 fusion.59
  234.1 147.3 %all-gather.13.cloned.1.call-done = bf16[1024,4096]{1,0:T(8,128)(2,1)} async-done(((bf16[256,4096]{1,0:T(8,128)(2,1)}), bf16[1024,4096]{1,0:T(8,128)(2,1)}) %all-gather.13.cloned.1.call-update) | async-done | bytes 8388624 | tf_op jit(solution)/shard_map/all_gather | solution.py:111
  381.4 8.5 convolution_add_fusion
  389.9 141.4 %all-gather.15.cloned.1.call-done = bf16[4096,1024]{1,0:T(8,128)(2,1)} async-done(((bf16[1024,1024]{1,0:T(8,128)(2,1)}), bf16[4096,1024]{1,0:T(8,128)(2,1)}) %all-gather.15.cloned.1.call-update) | async-done | bytes 8388624 | tf_op jit(solution)/shard_map/all_gather | solution.py:112
  531.3 9.1 fusion.61
  540.4 3.1 multiply_reduce_fusion.1
  544.1 1.0 copy-done.3
  545.1 1.7 convolution_convert_fusion.6
  546.8 2.2 copy.34
  549.0 8.5 fusion.9
  557.6 6.2 copy.37
  563.8 3.2 copy.46
  567.0 9.8 multiply_reduce_fusion
  576.8 6.6 multiply_convert_fusion
  583.4 2.9 convolution_convert_fusion.4
  586.4 6.2 copy.35
  592.6 3.1 copy.47
  595.8 4.1 convolution_convert_fusion.3
  600.4 5.6 fusion.60
  606.0 2.7 fusion.56
  608.7 2.2 copy.38
  610.9 5.2 reduce-scatter.25.cloned.1.call-done
  616.0 1.7 reshape_bitcast_fusion.1
  617.7 2.2 copy.36
  620.0 7.4 convolution_convert_fusion.2
  627.4 1.0 copy-done.15
  628.4 9.7 convolution_convert_fusion
  638.1 8.8 convolution_convert_fusion.1
  647.2 6.6 fusion.33
  655.7 7.2 reduce-scatter.17.cloned.1.call-done
  662.8 112.4 %reduce-scatter.15.cloned.1.call-done = bf16[256,3072]{1,0:T(8,128)(2,1)} async-done(((bf16[1024,3072]{1,0:T(8,128)(2,1)}), bf16[256,3072]{1,0:T(8,128)(2,1)}) %reduce-scatter.15.cloned.1.call-update) | async-done | bytes 1572880 | tf_op jit(solution)/shard_map/reduce_scatter | solution.py:236
  775.2 147.5 %reduce-scatter.21.cloned.1.call-done = bf16[1024,1024]{1,0:T(8,128)(2,1)} async-done(((bf16[4096,1024]{1,0:T(8,128)(2,1)}), bf16[1024,1024]{1,0:T(8,128)(2,1)}) %reduce-scatter.21.cloned.1.call-update) | async-done | bytes 2097168 | tf_op jit(solution)/shard_map/reduce_scatter | solution.py:245
  922.7 147.6 %reduce-scatter.19.cloned.1.call-done = bf16[256,4096]{1,0:T(8,128)(2,1)} async-done(((bf16[1024,4096]{1,0:T(8,128)(2,1)}), bf16[256,4096]{1,0:T(8,128)(2,1)}) %reduce-scatter.19.cloned.1.call-update) | async-done | bytes 2097168 | tf_op jit(solution)/shard_map/reduce_scatter | solution.py:242
  1072.1 11.4 all-reduce
  1083.6 8.6 fusion.25
  1092.2 1.3 fusion.41
  1093.5 0.9 copy.40
  1094.5 18.9 %reduce-scatter.23.cloned.1.call-done = bf16[6,256]{1,0:T(8,128)(2,1)} async-done(((bf16[6,1024]{1,0:T(8,128)(2,1)}), bf16[6,256]{1,0:T(8,128)(2,1)}) %reduce-scatter.23.cloned.1.call-update) | async-done | bytes 3088 | tf_op jit(solution)/shard_map/reduce_scatter | solution.py:251
  1113.4 14.1 %all-reduce.1 = (bf16[2,256]{1,0:T(2,128)(2,1)S(1)}, bf16[6,256]{1,0:T(8,128)(2,1)S(1)}, bf16[1024]{0:T(1024)(128)(2,1)S(1)}) all-reduce(bf16[2,256]{1,0:T(2,128)(2,1)S(1)} %copy.40, bf16[6,256]{1,0:T(8,128)(2,1)} %reduce-scatter.23.cloned.1.call-done, ...), channel_id=1, replica_groups=mesh['rep'=4,'fsdp'=4,'seq'=2] {'rep','seq'}, use_global_device_ids=true, to_apply=%region_24.25 | all-reduce | flops 3072 | bytes 12288 | tf_op jit(solution)/shard_map/psum | solution.py:263
  1129.2 91.0 %all-reduce.5.cloned.1.call-done = (bf16[256,3072]{1,0:T(8,128)(2,1)}, bf16[256,1024]{1,0:T(8,128)(2,1)}, bf16[256,4096]{1,0:T(8,128)(2,1)}, bf16[1024,1024]{1,0:T(8,128)(2,1)}) async-done(((bf16[256,3072]{1,0:T(8,128)(2,1)}, bf16[256,1024]{1,0:T(8,128)(2,1)}, bf16[256,4096]{1,0:T(8,128)(2,1)}, bf16[1024,1024]{1,0:T(8,128)(2,1)}), (bf16[256,3072]{1,0:T(8,128)(2,1)}, bf16[256,1024]{1,0:T(8,128)(2,1)}, ...) | async-done | bytes 6291472 | tf_op jit(solution)/shard_map/psum | solution.py:259
  1220.3 2.2 convert_element_type.248
  1222.5 2.0 convert_element_type.246
  1224.7 2.5 convert_element_type.250
  1227.2 2.5 convert_element_type.252
  (113 shorter events, 8.3 us)
Async XLA Ops:
  7.2 3.5 copy-start.19
  7.2 3.5 copy-start.17
  7.2 30.4 %copy-start.2 = (bf16[1,296,1024]{2,1,0:T(8,128)(2,1)S(1)}, bf16[1,296,1024]{2,1,0:T(8,128)(2,1)}, u32[]{:S(2)}) copy-start(bf16[1,296,1024]{2,1,0:T(8,128)(2,1)} %param.10) | copy-start | bytes 1818628
  7.2 121.7 %all-gather.9.cloned.1.call-start = ((), (), s32[]{:S(2)}) async-start(), calls=%async_computation.8 | async-start | bytes 7864320 | tf_op jit(solution)/shard_map/all_gather | solution.py:109
  10.6 151.2 %all-gather.19.cloned.1.call-start = ((), (), s32[]{:S(2)}) async-start(), calls=%async_computation.18 | async-start | bytes 1818624 | tf_op jit(solution)/shard_map/all_gather | solution.py:144
  134.0 1.8 copy-start.8
  136.7 46.9 %all-gather.17.cloned.1.call-start = ((), (), s32[]{:S(2)}) async-start(), calls=%async_computation.17 | async-start | bytes 1818624 | tf_op jit(solution)/shard_map/all_gather | solution.py:145
  136.8 3.0 copy-start.13
  139.7 91.3 %all-gather.11.cloned.1.call-start = ((), (), s32[]{:S(2)}) async-start(), calls=%async_computation.9 | async-start | bytes 2621440 | tf_op jit(solution)/shard_map/all_gather | solution.py:110
  140.7 240.7 %all-gather.13.cloned.1.call-start = ((), (), s32[]{:S(2)}) async-start(), calls=%async_computation.10 | async-start | bytes 10485760 | tf_op jit(solution)/shard_map/all_gather | solution.py:111
  144.8 386.4 %all-gather.15.cloned.1.call-start = ((), (), s32[]{:S(2)}) async-start(), calls=%async_computation.11 | async-start | bytes 10485760 | tf_op jit(solution)/shard_map/all_gather | solution.py:112
  148.7 0.7 copy-start.18
  148.7 457.3 %reduce-scatter.27.cloned.1.call-start = ((), (), s32[]{:S(2)}) async-start(), calls=%async_computation.20 | async-start | bytes 1818624
  161.7 24.3 %copy-start.5 = (bf16[296,1024]{0,1:T(8,128)(2,1)}, bf16[296,1024]{0,1:T(8,128)(2,1)S(1)}, u32[]{:S(2)}) copy-start(bf16[296,1024]{0,1:T(8,128)(2,1)S(1)} %copy.32) | copy-start | bytes 1818628
  188.2 4.9 copy-start
  188.2 4.9 copy-start.7
  531.3 9.1 copy-start.20
  540.3 3.1 copy-start.22
  540.3 3.1 copy-start.14
  543.5 1.6 copy-start.11
  544.1 1.0 copy-start.3
  567.0 49.1 %reduce-scatter.25.cloned.1.call-start = ((), (), s32[]{:S(2)}) async-start(), calls=%async_computation.19 | async-start | bytes 1818624
  576.8 6.6 copy-start.6
  583.4 3.0 copy-start.1
  595.8 67.0 %reduce-scatter.17.cloned.1.call-start = ((), (), s32[]{:S(2)}) async-start(), calls=%async_computation.13 | async-start | bytes 2621440 | tf_op jit(solution)/shard_map/reduce_scatter | solution.py:239
  600.0 175.2 %reduce-scatter.15.cloned.1.call-start = ((), (), s32[]{:S(2)}) async-start(), calls=%async_computation.12 | async-start | bytes 7864320 | tf_op jit(solution)/shard_map/reduce_scatter | solution.py:236
  627.3 1.1 copy-start.15
  627.4 295.3 %reduce-scatter.21.cloned.1.call-start = ((), (), s32[]{:S(2)}) async-start(), calls=%async_computation.15 | async-start | bytes 10485760 | tf_op jit(solution)/shard_map/reduce_scatter | solution.py:245
  638.1 432.1 %reduce-scatter.19.cloned.1.call-start = ((), (), s32[]{:S(2)}) async-start(), calls=%async_computation.14 | async-start | bytes 10485760 | tf_op jit(solution)/shard_map/reduce_scatter | solution.py:242
  647.0 446.6 %reduce-scatter.29.cloned.1.call-start = ((), (), s32[]{:S(2)}) async-start(), calls=%async_computation.21 | async-start | bytes 327680
  654.7 458.6 %reduce-scatter.23.cloned.1.call-start = ((), (), s32[]{:S(2)}) async-start(), calls=%async_computation.16 | async-start | bytes 20480 | tf_op jit(solution)/shard_map/reduce_scatter | solution.py:251
  655.6 564.7 %all-reduce.5.cloned.1.call-start = ((), (), s32[]{:S(2)}) async-start(), calls=%async_computation.22 | async-start | bytes 12582912 | tf_op jit(solution)/shard_map/psum | solution.py:259
  1070.2 0.7 copy-start.21
  1083.5 8.7 copy-start.16
  1083.5 8.7 copy-start.4
  1092.2 21.2 %dynamic-slice-start = ((bf16[4096]{0:T(1024)(128)(2,1)}, u32[]{:T(128)}), bf16[1024]{0:T(1024)(128)(2,1)S(1)}, s32[]{:S(2)}) async-start(bf16[4096]{0:T(1024)(128)(2,1)} %copy-done.16, u32[]{:T(128)} %multiply.49), calls=%async_computation.23 | async-start | bytes 4608
  1220.3 2.2 copy-start.12
  1222.5 2.2 copy-start.10
  1224.7 2.5 copy-start.9
Sparse Core Ops, SparseCore 0:
  10.7 118.1 all-gather.8
  136.8 21.4 all-gather.18
  160.4 23.1 all-gather.16
  185.0 45.9 all-gather.10
  233.0 148.3 all-gather.12
  383.4 147.8 all-gather.14
  567.1 20.3 reduce-scatter.26
  595.9 20.0 reduce-scatter.24
  618.9 43.8 reduce-scatter.16
  665.1 110.0 reduce-scatter.14
  777.6 144.9 reduce-scatter.20
  925.0 145.1 reduce-scatter.18
  1073.2 20.3 reduce-scatter.28
  1096.2 17.1 reduce-scatter.22
  1117.3 102.9 all-reduce.4
where the time goes:
time: 1240 us
  waiting for transfers between devices  963 us (78%)
  matrix products  109 us (9%)
  blocking collectives  64.3 us (5%)
  local copies, waits for them, and re-layouts  42.4 us (3%)
  other arithmetic  41.2 us (3%)
  between operations  15.9 us (1%)
    reduce_scatter x1, waiting for transfers between devices, on_device(): lax.psum_scatter(grad_fc1.astype(jnp.bfloat16), 'fsdp', scatter_dimension...  148 us
    reduce_scatter x1, waiting for transfers between devices, on_device(): lax.psum_scatter(grad_fc2.astype(jnp.bfloat16), 'fsdp', scatter_dimension...  148 us
    all_gather x1, waiting for transfers between devices, on_device(): lax.all_gather(low_fc1, 'fsdp', axis=0, tiled=True)  147 us
    all_gather x1, waiting for transfers between devices, on_device(): lax.all_gather(low_fc2, 'fsdp', axis=0, tiled=True)  141 us
    reduce_scatter x1, waiting for transfers between devices, on_device(): lax.psum_scatter(grad_qkv.astype(jnp.bfloat16), 'fsdp', scatter_dimension...  112 us
    psum x1, waiting for transfers between devices, on_device(): lax.psum(shards[0].astype(jnp.bfloat16), ('rep', 'seq')).astype(jnp.float32)  91 us
    all_gather x1, waiting for transfers between devices, on_device(): lax.all_gather(low_qkv, 'fsdp', axis=0, tiled=True)  90.8 us
    unnamed x58, local copies, waits for them, and re-layouts  33.7 us
  transfers between devices with their start and end apart: 15, of which 12 were waited for; matrix products, arithmetic and copies ran while one was open for 11% of the time, Pallas kernels for 0%

commit v1 on v0

--- a/solution.py
+++ b/solution.py
@@ -8,6 +8,16 @@
 IMG_TOK = 577
 EPSILON = 1e-05
 NEGATIVE = -1e30
+
+
+def ring_gather(x, axis, dim):
+    ways, here, turn = (lax.axis_size(axis), lax.axis_index(axis), x.shape[dim])
+    shape = [n * ways if d == dim else n for d, n in enumerate(x.shape)]
+    full = lax.dynamic_update_slice_in_dim(jnp.zeros(shape, x.dtype), x, here * turn, axis=dim)
+    for far in range(1, ways):
+        x = lax.ppermute(x, axis, [(d, (d + 1) % ways) for d in range(ways)])
+        full = lax.dynamic_update_slice_in_dim(full, x, (here - far) % ways * turn, axis=dim)
+    return full
 
 
 def normalize(inputs, gain_row, shift_row):
@@ -109,7 +119,7 @@
         lax.all_gather(low_qkv, "fsdp", axis=0, tiled=True),
         lax.all_gather(low_out, "fsdp", axis=0, tiled=True),
         lax.all_gather(low_fc1, "fsdp", axis=0, tiled=True),
-        lax.all_gather(low_fc2, "fsdp", axis=0, tiled=True),
+        ring_gather(low_fc2, "fsdp", 0),
         lax.all_gather(low_gains, "fsdp", axis=1, tiled=True),
         lax.all_gather(low_biases, "fsdp", axis=1, tiled=True),
         lax.all_gather(low_fc1_bias, "fsdp", axis=0, tiled=True),

time: 1240 us -> 1360 us (1.097)
  waiting for transfers between devices: 963 us -> 1040 us
  starting transfers between devices: 1.2 us -> 23.5 us
  local copies, waits for them, and re-layouts: 42.4 us -> 58.1 us
    ppermute x0 -> x3, waiting for transfers between devices: none -> 176 us  [ring_gather(): x = lax.ppermute(x, axis, [(d, (d + 1) % ways) for d in range(ways)])]
    reduce_scatter x1, waiting for transfers between devices: 112 us -> 2.37 us  [on_device(): lax.psum_scatter(grad_qkv.astype(jnp.bfloat16), 'fsdp', scatter_dimension...]
    reduce_scatter x1, waiting for transfers between devices: 148 us -> 177 us  [on_device(): lax.psum_scatter(grad_fc1.astype(jnp.bfloat16), 'fsdp', scatter_dimension...]
    ppermute x0 -> x3, starting transfers between devices: none -> 22.5 us  [ring_gather(): x = lax.ppermute(x, axis, [(d, (d + 1) % ways) for d in range(ways)])]
    all_gather x1, waiting for transfers between devices: 19.9 us -> 0.02 us  [on_device(): lax.all_gather(values_local, 'seq', axis=1, tiled=True)]
    all_gather x1, waiting for transfers between devices: 0.02 us -> 16.7 us  [on_device(): lax.all_gather(keys_local, 'seq', axis=1, tiled=True)]
    unnamed x58 -> x62, local copies, waits for them, and re-layouts: 33.7 us -> 34.6 us
  transfers between devices with their start and end apart: 15 -> 18, of which waited for: 12 -> 13; matrix products, arithmetic and copies ran while one was open for 11% -> 11% of each run, Pallas kernels for 0% -> 0%
where the time goes in v1:
time: 1360 us; the launch traced here: 1350 us
  waiting for transfers between devices  1040 us (76%)
  matrix products  109 us (8%)
  blocking collectives  64.6 us (5%)
  local copies, waits for them, and re-layouts  58.1 us (4%)
  other arithmetic  38.7 us (3%)
  starting transfers between devices  23.5 us (2%)
  between operations  16 us (1%)
    reduce_scatter x1, waiting for transfers between devices, on_device(): lax.psum_scatter(grad_fc1.astype(jnp.bfloat16), 'fsdp', scatter_dimension...  177 us
    ppermute x3, waiting for transfers between devices, ring_gather(): x = lax.ppermute(x, axis, [(d, (d + 1) % ways) for d in range(ways)])  176 us
    all_gather x1, waiting for transfers between devices, on_device(): lax.all_gather(low_fc1, 'fsdp', axis=0, tiled=True)  147 us
    reduce_scatter x1, waiting for transfers between devices, on_device(): lax.psum_scatter(grad_fc2.astype(jnp.bfloat16), 'fsdp', scatter_dimension...  146 us
    all_gather x1, waiting for transfers between devices, on_device(): lax.all_gather(low_fc2, 'fsdp', axis=0, tiled=True)  141 us
    psum x1, waiting for transfers between devices, on_device(): lax.psum(shards[0].astype(jnp.bfloat16), ('rep', 'seq')).astype(jnp.float32)  91.1 us
    all_gather x1, waiting for transfers between devices, on_device(): lax.all_gather(low_qkv, 'fsdp', axis=0, tiled=True)  90.8 us
    all_gather x1, waiting for transfers between devices, on_device(): lax.all_gather(low_out, 'fsdp', axis=0, tiled=True)  34.9 us
  transfers between devices with their start and end apart: 18, of which 13 were waited for; matrix products, arithmetic and copies ran while one was open for 11% of the time, Pallas kernels for 0%

profile of v1, /device:TPU:0, one launch (start us, length us, event | category | flops | bytes accessed | tf_op | source)
XLA Modules:
  0.0 1347.9 jit_solution(11977238436621204758)
XLA Ops:
  7.3 3.3 convert_element_type.215
  10.7 12.6 all_gather.31
  23.3 14.3 %all_gather.32 = bf16[6,1024]{1,0:T(8,128)(2,1)S(1)} all-gather(bf16[6,256]{1,0:T(8,128)(2,1)S(1)} %convert_element_type.212), channel_id=1, replica_groups=mesh['rep'=4,'fsdp'=4,'seq'=2] {'fsdp'}, dimensions={1}, use_global_device_ids=true | all-gather | bytes 15360 | tf_op jit(solution)/shard_map/all_gather | solution.py:124
  38.1 90.8 %all-gather.9.cloned.1.call-done = bf16[1024,3072]{1,0:T(8,128)(2,1)} async-done(((bf16[256,3072]{1,0:T(8,128)(2,1)}), bf16[1024,3072]{1,0:T(8,128)(2,1)}) %all-gather.9.cloned.1.call-update) | async-done | bytes 6291472 | tf_op jit(solution)/shard_map/all_gather | solution.py:119
  128.9 5.0 fusion.53
  134.0 1.8 copy-done.9
  137.0 2.2 slice.67
  140.2 4.1 convert_element_type.224
  144.4 4.3 broadcast_in_dim.64
  148.8 2.7 constant_dynamic-update-slice_fusion.3
  152.2 11.9 all_gather.38
  164.5 2.7 copy.31
  167.2 16.7 %all-gather.19.cloned.1.call-done = bf16[592,1024]{1,0:T(8,128)(2,1)} async-done(((bf16[296,1024]{1,0:T(8,128)(2,1)}), bf16[592,1024]{1,0:T(8,128)(2,1)}) %all-gather.19.cloned.1.call-update) | async-done | bytes 1212432 | tf_op jit(solution)/shard_map/all_gather | solution.py:154
  183.8 1.7 copy.33
  185.5 2.2 select_reduce_fusion
  187.8 3.2 fusion
  192.4 4.5 fusion.20
  197.0 34.9 %all-gather.11.cloned.1.call-done = bf16[1024,1024]{1,0:T(8,128)(2,1)} async-done(((bf16[256,1024]{1,0:T(8,128)(2,1)}), bf16[1024,1024]{1,0:T(8,128)(2,1)}) %all-gather.11.cloned.1.call-update) | async-done | bytes 2097168 | tf_op jit(solution)/shard_map/all_gather | solution.py:120
  231.9 2.8 fusion.59
  235.0 147.2 %all-gather.13.cloned.1.call-done = bf16[1024,4096]{1,0:T(8,128)(2,1)} async-done(((bf16[256,4096]{1,0:T(8,128)(2,1)}), bf16[1024,4096]{1,0:T(8,128)(2,1)}) %all-gather.13.cloned.1.call-update) | async-done | bytes 8388624 | tf_op jit(solution)/shard_map/all_gather | solution.py:121
  382.2 8.5 convolution_add_fusion
  390.7 141.4 %all-gather.15.cloned.1.call-done = bf16[4096,1024]{1,0:T(8,128)(2,1)} async-done(((bf16[1024,1024]{1,0:T(8,128)(2,1)}), bf16[4096,1024]{1,0:T(8,128)(2,1)}) %all-gather.15.cloned.1.call-update) | async-done | bytes 8388624 | tf_op jit(solution)/shard_map/all_gather | solution.py:173
  532.1 9.1 fusion.61
  541.2 3.1 multiply_reduce_fusion.1
  545.9 1.7 convolution_convert_fusion.6
  547.6 2.2 copy.34
  549.8 8.5 fusion.9
  558.4 6.2 copy.37
  564.6 3.2 copy.46
  567.8 9.8 multiply_reduce_fusion
  577.6 6.6 multiply_convert_fusion
  584.2 2.9 convolution_convert_fusion.4
  587.2 6.2 copy.35
  593.4 3.2 copy.47
  596.7 4.1 convolution_convert_fusion.3
  601.2 5.5 fusion.60
  606.8 2.7 fusion.56
  609.4 2.2 copy.38
  611.6 5.2 reduce-scatter.25.cloned.1.call-done
  616.8 1.7 reshape_bitcast_fusion.1
  618.5 2.2 copy.36
  620.8 7.4 convolution_convert_fusion.2
  628.3 8.8 convolution_convert_fusion.1
  638.1 9.6 convolution_convert_fusion
  647.8 1.6 collective-permute-start
  649.3 81.1 %collective-permute-done = bf16[1024,1024]{1,0:T(8,128)(2,1)S(1)} collective-permute-done((bf16[1024,1024]{1,0:T(8,128)(2,1)}, bf16[1024,1024]{1,0:T(8,128)(2,1)S(1)}, u32[]{:S(2)}, u32[]{:S(2)}) %collective-permute-start) | collective-permute-done | bytes 2097184 | tf_op jit(solution)/shard_map/ppermute | solution.py:18
  731.7 17.3 %collective-permute-start.1 = (bf16[1024,1024]{1,0:T(8,128)(2,1)S(1)}, bf16[1024,1024]{1,0:T(8,128)(2,1)}, u32[]{:S(2)}, u32[]{:S(2)}) collective-permute-start(bf16[1024,1024]{1,0:T(8,128)(2,1)S(1)} %collective-permute-done), channel_id=1, source_target_pairs={{0,2},{2,4},{4,6},{6,0},{1,3},{3,5},{5,7},{7,1},{8,10},{10,12},{12... | collective-permute-start | bytes 6291464 | tf_op jit(solution)/shard_map/ppermute | solution.py:18
  749.0 94.7 %collective-permute-done.1 = bf16[1024,1024]{1,0:T(8,128)(2,1)} collective-permute-done((bf16[1024,1024]{1,0:T(8,128)(2,1)S(1)}, bf16[1024,1024]{1,0:T(8,128)(2,1)}, u32[]{:S(2)}, u32[]{:S(2)}) %collective-permute-start.1) | collective-permute-done | bytes 2097184 | tf_op jit(solution)/shard_map/ppermute | solution.py:18
  843.8 3.6 collective-permute-start.2
  847.3 6.5 fusion.33
  855.8 2.4 reduce-scatter.15.cloned.1.call-done
  858.1 177.2 %reduce-scatter.19.cloned.1.call-done = bf16[256,4096]{1,0:T(8,128)(2,1)} async-done(((bf16[1024,4096]{1,0:T(8,128)(2,1)}), bf16[256,4096]{1,0:T(8,128)(2,1)}) %reduce-scatter.19.cloned.1.call-update) | async-done | bytes 2097168 | tf_op jit(solution)/shard_map/reduce_scatter | solution.py:252
  1035.4 145.7 %reduce-scatter.21.cloned.1.call-done = bf16[1024,1024]{1,0:T(8,128)(2,1)} async-done(((bf16[4096,1024]{1,0:T(8,128)(2,1)}), bf16[1024,1024]{1,0:T(8,128)(2,1)}) %reduce-scatter.21.cloned.1.call-update) | async-done | bytes 2097168 | tf_op jit(solution)/shard_map/reduce_scatter | solution.py:255
  1183.0 3.1 constant_dynamic-update-slice_fusion.2
  1186.0 3.1 constant_dynamic-update-slice_fusion.1
  1189.1 3.1 constant_dynamic-update-slice_fusion
  1192.2 11.7 all-reduce
  1204.0 8.6 fusion.25
  1214.8 9.7 reduce-scatter.23.cloned.1.call-done
  1224.5 14.1 %all-reduce.1 = (bf16[2,256]{1,0:T(2,128)(2,1)S(1)}, bf16[6,256]{1,0:T(8,128)(2,1)S(1)}, bf16[1024]{0:T(1024)(128)(2,1)S(1)}) all-reduce(bf16[2,256]{1,0:T(2,128)(2,1)S(1)} %copy.40, bf16[6,256]{1,0:T(8,128)(2,1)} %reduce-scatter.23.cloned.1.call-done, ...), channel_id=1, replica_groups=mesh['rep'=4,'fsdp'=4,'seq'=2] {'rep','seq'}, use_global_device_ids=true, to_apply=%region_24.25 | all-reduce | flops 3072 | bytes 12288 | tf_op jit(solution)/shard_map/psum | solution.py:273
  1240.4 91.1 %all-reduce.5.cloned.1.call-done = (bf16[256,3072]{1,0:T(8,128)(2,1)}, bf16[256,1024]{1,0:T(8,128)(2,1)}, bf16[256,4096]{1,0:T(8,128)(2,1)}, bf16[1024,1024]{1,0:T(8,128)(2,1)}) async-done(((bf16[256,3072]{1,0:T(8,128)(2,1)}, bf16[256,1024]{1,0:T(8,128)(2,1)}, bf16[256,4096]{1,0:T(8,128)(2,1)}, bf16[1024,1024]{1,0:T(8,128)(2,1)}), (bf16[256,3072]{1,0:T(8,128)(2,1)}, bf16[256,1024]{1,0:T(8,128)(2,1)}, ...) | async-done | bytes 6291472 | tf_op jit(solution)/shard_map/psum | solution.py:269
  1331.5 3.6 convert_element_type.246
  1336.2 2.5 convert_element_type.250
  1338.7 2.5 convert_element_type.252
  (127 shorter events, 18.0 us)
Async XLA Ops:
  7.2 3.5 copy-start.19
  7.2 3.5 copy-start.21
  7.2 30.4 %copy-start.2 = (bf16[1,296,1024]{2,1,0:T(8,128)(2,1)S(1)}, bf16[1,296,1024]{2,1,0:T(8,128)(2,1)}, u32[]{:S(2)}) copy-start(bf16[1,296,1024]{2,1,0:T(8,128)(2,1)} %param.10) | copy-start | bytes 1818628
  7.2 121.7 %all-gather.9.cloned.1.call-start = ((), (), s32[]{:S(2)}) async-start(), calls=%async_computation.8 | async-start | bytes 7864320 | tf_op jit(solution)/shard_map/all_gather | solution.py:119
  10.6 153.9 %all-gather.17.cloned.1.call-start = ((), (), s32[]{:S(2)}) async-start(), calls=%async_computation.17 | async-start | bytes 1818624 | tf_op jit(solution)/shard_map/all_gather | solution.py:155
  134.0 1.8 copy-start.9
  135.8 3.5 copy-start.14
  137.0 46.9 %all-gather.19.cloned.1.call-start = ((), (), s32[]{:S(2)}) async-start(), calls=%async_computation.18 | async-start | bytes 1818624 | tf_op jit(solution)/shard_map/all_gather | solution.py:154
  139.2 92.6 %all-gather.11.cloned.1.call-start = ((), (), s32[]{:S(2)}) async-start(), calls=%async_computation.9 | async-start | bytes 2621440 | tf_op jit(solution)/shard_map/all_gather | solution.py:120
  140.2 242.0 %all-gather.13.cloned.1.call-start = ((), (), s32[]{:S(2)}) async-start(), calls=%async_computation.10 | async-start | bytes 10485760 | tf_op jit(solution)/shard_map/all_gather | solution.py:121
  144.3 387.7 %all-gather.15.cloned.1.call-start = ((), (), s32[]{:S(2)}) async-start(), calls=%async_computation.11 | async-start | bytes 10485760 | tf_op jit(solution)/shard_map/all_gather | solution.py:173
  144.4 4.4 copy-start.8
  148.7 3.4 copy-start.20
  151.5 455.3 %reduce-scatter.27.cloned.1.call-start = ((), (), s32[]{:S(2)}) async-start(), calls=%async_computation.20 | async-start | bytes 1818624
  164.4 21.1 %copy-start.5 = (bf16[296,1024]{0,1:T(8,128)(2,1)}, bf16[296,1024]{0,1:T(8,128)(2,1)S(1)}, u32[]{:S(2)}) copy-start(bf16[296,1024]{0,1:T(8,128)(2,1)S(1)} %copy.32) | copy-start | bytes 1818628
  187.8 4.7 copy-start
  187.8 4.7 copy-start.7
  532.1 9.1 copy-start.22
  541.1 3.1 copy-start.24
  541.2 3.1 copy-start.15
  544.3 1.7 copy-start.13
  544.9 1.1 copy-start.3
  567.8 49.1 %reduce-scatter.25.cloned.1.call-start = ((), (), s32[]{:S(2)}) async-start(), calls=%async_computation.19 | async-start | bytes 1818624
  577.6 6.6 copy-start.6
  584.2 3.0 copy-start.1
  596.6 259.2 %reduce-scatter.17.cloned.1.call-start = ((), (), s32[]{:S(2)}) async-start(), calls=%async_computation.13 | async-start | bytes 2621440 | tf_op jit(solution)/shard_map/reduce_scatter | solution.py:249
  600.8 257.4 %reduce-scatter.15.cloned.1.call-start = ((), (), s32[]{:S(2)}) async-start(), calls=%async_computation.12 | async-start | bytes 7864320 | tf_op jit(solution)/shard_map/reduce_scatter | solution.py:246
  628.2 407.1 %reduce-scatter.19.cloned.1.call-start = ((), (), s32[]{:S(2)}) async-start(), calls=%async_computation.14 | async-start | bytes 10485760 | tf_op jit(solution)/shard_map/reduce_scatter | solution.py:252
  637.1 1.1 copy-start.16
  637.1 544.0 %reduce-scatter.21.cloned.1.call-start = ((), (), s32[]{:S(2)}) async-start(), calls=%async_computation.15 | async-start | bytes 10485760 | tf_op jit(solution)/shard_map/reduce_scatter | solution.py:255
  647.7 566.2 %reduce-scatter.29.cloned.1.call-start = ((), (), s32[]{:S(2)}) async-start(), calls=%async_computation.21 | async-start | bytes 327680
  647.8 82.7 %collective-permute-start = (bf16[1024,1024]{1,0:T(8,128)(2,1)}, bf16[1024,1024]{1,0:T(8,128)(2,1)S(1)}, u32[]{:S(2)}, u32[]{:S(2)}) collective-permute-start(bf16[1024,1024]{1,0:T(8,128)(2,1)} %get-tuple-element.74), channel_id=1, source_target_pairs={{0,2},{2,4},{4,6},{6,0},{1,3},{3,5},{5,7},{7,1},{8,10},{10,12},{12... | collective-permute-start | bytes 6291464 | tf_op jit(solution)/shard_map/ppermute | solution.py:18
  730.4 1.3 copy-start.12
  731.7 112.0 %collective-permute-start.1 = (bf16[1024,1024]{1,0:T(8,128)(2,1)S(1)}, bf16[1024,1024]{1,0:T(8,128)(2,1)}, u32[]{:S(2)}, u32[]{:S(2)}) collective-permute-start(bf16[1024,1024]{1,0:T(8,128)(2,1)S(1)} %collective-permute-done), channel_id=1, source_target_pairs={{0,2},{2,4},{4,6},{6,0},{1,3},{3,5},{5,7},{7,1},{8,10},{10,12},{12... | collective-permute-start | bytes 6291464 | tf_op jit(solution)/shard_map/ppermute | solution.py:18
  843.8 345.3 %collective-permute-start.2 = (bf16[1024,1024]{1,0:T(8,128)(2,1)}, bf16[1024,1024]{1,0:T(8,128)(2,1)}, u32[]{:S(2)}, u32[]{:S(2)}) collective-permute-start(bf16[1024,1024]{1,0:T(8,128)(2,1)} %collective-permute-done.1), channel_id=1, source_target_pairs={{0,2},{2,4},{4,6},{6,0},{1,3},{3,5},{5,7},{7,1},{8,10},{10,12},{12... | collective-permute-start | bytes 6291464 | tf_op jit(solution)/shard_map/ppermute | solution.py:18
  854.8 369.7 %reduce-scatter.23.cloned.1.call-start = ((), (), s32[]{:S(2)}) async-start(), calls=%async_computation.16 | async-start | bytes 20480 | tf_op jit(solution)/shard_map/reduce_scatter | solution.py:261
  855.7 475.8 %all-reduce.5.cloned.1.call-start = ((), (), s32[]{:S(2)}) async-start(), calls=%async_computation.22 | async-start | bytes 12582912 | tf_op jit(solution)/shard_map/psum | solution.py:269
  1181.1 0.7 copy-start.23
  1203.9 8.7 copy-start.18
  1204.0 8.7 copy-start.4
  1212.6 12.0 dynamic-slice-start
  1331.5 3.6 copy-start.17
  1331.5 4.7 copy-start.11
  1336.2 2.5 copy-start.10
Sparse Core Ops, SparseCore 0:
  10.7 118.1 all-gather.8
  137.1 21.4 all-gather.16
  160.7 23.1 all-gather.18
  185.8 45.9 all-gather.10
  233.9 148.2 all-gather.12
  384.2 147.8 all-gather.14
  567.9 20.3 reduce-scatter.26
  596.7 20.0 reduce-scatter.24
  619.1 52.8 reduce-scatter.16
  674.3 183.8 reduce-scatter.14
  860.6 174.6 reduce-scatter.18
  1037.7 143.3 reduce-scatter.20
  1184.0 20.7 reduce-scatter.28
  1207.4 17.0 reduce-scatter.22
  1228.4 103.0 all-reduce.4
